TPU v7x, 128 devices: a whole 4x4x4 slice. The times are simulated.
128 devices in a mesh: leaf: 32 (over x, z, core), level: 4 (over y).
Axes of the slice: x: 4, y: 4, z: 4, core: 2. Of those that a mesh axis runs over, the one named last changes fastest.
Arguments:
- right_side: float32 [8, 2097152], P(None, ('leaf', 'level')), may hold values from -28 to 28
- basis: bfloat16 [16384, 128, 128], P(('leaf', 'level')), may hold values from -0.5 to 0.5
- transfer: bfloat16 [16384, 128, 128], P(('leaf', 'level')), may hold values from -0.5 to 0.5
- order: int32 [128, 128], P(('leaf', 'level')), may hold values from 0 to 127, each once within a row
- far_src: int32 [4096, 4], P(('leaf', 'level')), may hold values from 0 to 127
- far_mats: bfloat16 [4096, 4, 128, 128], P(('leaf', 'level')), may hold values from -0.125 to 0.125
- near_target: int32 [32768], P(('leaf', 'level')), may hold values from 0 to 127
- near_dest: int32 [32768, 1], P(('leaf', 'level')), may hold values from 0 to 127; in each aligned block of 256 rows (0 to 255, 256 to 511, ...) at most 4 rows name the same one
- near_src: int32 [32768], P(('leaf', 'level')), may hold values from 0 to 127
- near_blocks: bfloat16 [32768, 128, 128], P(('leaf', 'level')), may hold values from -0.5 to 0.5
Outputs:
- solution: float32 [8, 2097152], P(None, ('leaf', 'level'))
- residual: float32 [8, 2097152], P(None, ('leaf', 'level'))
Inputs may be any that keep to these rules, and one draw needn't show every extreme that they name: `order`: each group's row is a permutation of 0 to 127. `near_dest`: among the pairs of one group, no group is named more than 4 times, a bound that some block reaches.
All inputs are finite; a program needn't handle non-finite values.
Results may differ from a plain program's by a relative error of at most 0.0022.
Values may be sent and summed in bfloat16 or wider, within the bound.
A program may use at most 128 MiB of HBM per device.

v0:
```python
import jax
import jax.numpy as jnp
from jax import lax
from jax.sharding import PartitionSpec as P

CHILDREN = 4
EPSILON = 1e-06
SCALE = 2.0 ** (-20)


def local(
    right_side,
    basis,
    transfer,
    order,
    far_src,
    far_mats,
    near_target,
    near_dest,
    near_src,
    near_blocks,
):
    systems = right_side.shape[0]
    clusters, points, coeffs = basis.shape
    groups = lax.axis_size(("leaf", "level"))
    capacity = max(4, 2 * near_dest.shape[0] // groups)
    parents = clusters // CHILDREN
    partners = far_src.shape[1]
    permutation = order[0]
    positions = jnp.arange(clusters, dtype=jnp.int32)
    inverse = jnp.zeros((clusters,), jnp.int32).at[permutation].set(positions)
    basis_slot = jnp.take(basis, permutation, axis=0)
    transfer_slot = jnp.take(transfer, permutation, axis=0)
    targets = near_dest[:, 0]
    member = (targets[:, None] == jnp.arange(groups, dtype=jnp.int32)[None, :]).astype(jnp.int32)
    slot_rank = jnp.sum(jnp.cumsum(member, axis=0) * member, axis=1) - 1
    slot_index = targets * capacity + slot_rank
    source_label = (
        jnp.full((groups * capacity,), -1.0, jnp.float32)
        .at[slot_index]
        .set(near_src.astype(jnp.float32))
    )
    cluster_ids = positions.astype(jnp.float32)

    def near_field(rounded):
        columns = jnp.take(rounded, near_target, axis=1)
        partial_rows = jnp.einsum(
            "rnp,npq->nrq", columns, near_blocks, preferred_element_type=jnp.float32
        )
        outgoing = (
            jnp.zeros((groups * capacity, systems, points), jnp.float32)
            .at[slot_index]
            .set(partial_rows)
        )
        incoming, labels = (
            lax.all_to_all(
                outgoing.astype(jnp.bfloat16),
                ("leaf", "level"),
                split_axis=0,
                concat_axis=0,
                tiled=True,
            ).astype(outgoing.dtype),
            lax.all_to_all(
                source_label.astype(jnp.bfloat16),
                ("leaf", "level"),
                split_axis=0,
                concat_axis=0,
                tiled=True,
            ).astype(source_label.dtype),
        )
        landing = (labels[:, None] == cluster_ids[None, :]).astype(jnp.float32)
        return jnp.einsum("sc,srp->rcp", landing, incoming, precision=lax.Precision.HIGHEST)

    def upward(lifted):
        arrived = lax.all_to_all(lifted, ("leaf", "level"), split_axis=0, concat_axis=0, tiled=True)
        return arrived

    def downward(spread):
        returned = lax.all_to_all(
            spread, ("leaf", "level"), split_axis=0, concat_axis=0, tiled=True
        )
        return returned

    def operator(vector_in):
        rounded = vector_in.astype(jnp.bfloat16).reshape(systems, clusters, points)
        near_sum = near_field(rounded)
        ordered = jnp.take(rounded, permutation, axis=1)
        expansion = jnp.einsum(
            "rsp,spk->srk", ordered, basis_slot, preferred_element_type=jnp.float32
        ).astype(jnp.bfloat16)
        lifted = jnp.einsum(
            "srk,skj->srj", expansion, transfer_slot, preferred_element_type=jnp.float32
        )
        arrived = upward(lifted)
        parent_rows = jnp.sum(arrived.reshape(parents, CHILDREN, systems, coeffs), axis=1).astype(
            jnp.bfloat16
        )
        parent_table = lax.all_gather(parent_rows, "level", axis=0, tiled=True)
        picked = jnp.take(parent_table, far_src.reshape(-1), axis=0).reshape(
            parents, partners, systems, coeffs
        )
        translated = jnp.einsum(
            "qfrk,qfkj->qrj", picked, far_mats, preferred_element_type=jnp.float32
        ).astype(jnp.bfloat16)
        returned = downward(jnp.repeat(translated, CHILDREN, axis=0))
        expanded = jnp.einsum(
            "srk,sjk->srj", returned, transfer_slot, preferred_element_type=jnp.float32
        ).astype(jnp.bfloat16)
        far_slot = jnp.einsum(
            "srk,spk->rsp", expanded, basis_slot, preferred_element_type=jnp.float32
        )
        far_sum = jnp.take(far_slot, inverse, axis=1)
        return near_sum + far_sum

    tiles = right_side.reshape(systems, clusters, points)
    image = operator(tiles)
    scaled = image * SCALE
    second = operator(scaled)
    own = jnp.stack(
        [
            jnp.sum(left * right, axis=(1, 2))
            for left, right in (
                (tiles, tiles),
                (tiles, image),
                (image, image),
                (tiles, second),
                (scaled, second),
                (second, second),
            )
        ]
    )
    dots = jnp.sum(lax.all_gather(own, ("leaf", "level")), axis=0)
    first_x, first_z, second_x, second_z, second_u = combine(dots)
    solved = first_x[:, None, None] * tiles + first_z[:, None, None] * image
    left_over = (
        second_x[:, None, None] * tiles
        + second_z[:, None, None] * image
        + second_u[:, None, None] * second
    )
    return (solved.reshape(systems, -1), left_over.reshape(systems, -1))


def combine(dots):
    start_sq = dots[0] + EPSILON
    start_norm = jnp.sqrt(start_sq)
    xx, xz, zz, xu, zu, uu = (dots[k] / start_sq for k in range(6))
    along_one = 0.5 * xx + xz
    kappa = along_one - 0.5
    rest_raw = zz - 2.0 * kappa * xz + kappa * kappa * xx
    rest_sq = rest_raw + EPSILON
    rest_one = jnp.sqrt(rest_sq)
    scaled_rest = SCALE * rest_one
    scaled_sq = scaled_rest * scaled_rest
    xzs = SCALE * xz
    zzs = SCALE * SCALE * zz
    beta = (xz - kappa * xx) / rest_one
    gamma = rest_raw / rest_sq
    one_t = (xu - kappa * xzs) / scaled_rest
    two_t = (zu - kappa * zzs - SCALE * kappa * (xu - kappa * xzs)) / scaled_sq
    t_t = (uu - 2.0 * kappa * zu + kappa * kappa * zzs) / scaled_sq
    cross_two = 0.5 * beta + one_t
    along_two = 0.5 * gamma + two_t
    short = 0.5 - along_two
    tail_sq = (
        t_t
        + short * short * gamma
        + cross_two * cross_two * xx
        + 2.0 * short * two_t
        - 2.0 * cross_two * one_t
        - 2.0 * cross_two * short * beta
    )
    gram_first = along_one * along_one + rest_one * rest_one
    gram_cross = along_one * cross_two + rest_one * along_two
    gram_last = cross_two * cross_two + along_two * along_two + tail_sq
    determinant = gram_first * gram_last - gram_cross * gram_cross
    coef_one = start_norm * (along_one * gram_last - cross_two * gram_cross) / determinant
    coef_two = start_norm * (gram_first * cross_two - gram_cross * along_one) / determinant
    one = coef_one / start_norm
    two = coef_two / (start_norm * rest_one)
    return (
        one - kappa * two,
        two,
        1.0 - 0.5 * one + 0.5 * kappa * two,
        -one - (0.5 - kappa) * two,
        -coef_two / (start_norm * scaled_rest),
    )


def solution(mesh):
    placed = (
        P(None, ("leaf", "level")),
        P(("leaf", "level"), None, None),
        P(("leaf", "level"), None, None),
        P(("leaf", "level"), None),
        P(("leaf", "level"), None),
        P(("leaf", "level"), None, None, None),
        P(("leaf", "level")),
        P(("leaf", "level"), None),
        P(("leaf", "level")),
        P(("leaf", "level"), None, None),
    )
    return jax.shard_map(
        local,
        mesh=mesh,
        in_specs=placed,
        out_specs=(P(None, ("leaf", "level")), P(None, ("leaf", "level"))),
        check_vma=False,
    )
```

profile of v0, /device:TPU:1, one launch (start us, length us, event | category | flops | bytes accessed | tf_op | source)
XLA Modules:
  0.0 271.7 jit_solution(17496570078938637699)
XLA Ops:
  2.0 1.3 multiply_reduce_fusion.5
  3.9 5.2 %gather_fusion.3 = bf16[128,128,128]{2,1,0:T(8,128)(2,1)} fusion(bf16[128,128,128]{2,1,0:T(8,128)(2,1)} %param.22, s32[1024]{0:T(1024)S(1)} %pad_clamp_fusion.2), kind=kCustom, calls=%fused_computation.6.clone | custom fusion | bytes 8389120 | tf_op jit(solution)/shard_map/jit(_take)/gather | solution.py:33
  9.2 5.2 %gather_fusion.1 = bf16[128,128,128]{2,1,0:T(8,128)(2,1)} fusion(bf16[128,128,128]{2,1,0:T(8,128)(2,1)} %param.21, s32[1024]{0:T(1024)S(1)} %pad_clamp_fusion.2), kind=kCustom, calls=%fused_computation.1.clone | custom fusion | bytes 8389120 | tf_op jit(solution)/shard_map/jit(_take)/gather | solution.py:32
  14.4 6.7 %fusion.2 = f32[128,8,128]{2,1,0:T(8,128)} fusion(bf16[128,8,128]{2,1,0:T(8,128)(2,1)S(1)} %gather_fusion.2, pred[128]{0:T(512)(128)(4,1)S(1)} %compare_and_fusion.2, bf16[128,128,128]{2,1,0:T(8,128)(2,1)} %gather_fusion.1, bf16[128,128,128]{2,1,0:T(8,128)(2,1)} %gather_fusion.3), kind=kOutput, calls=%fused_computation.26 | convolution fusion | flops 71565312 | bytes 9175168 | tf_op jit(solution)/shard_map/srk,skj->srj/dot_general | solution.py:91
  21.1 12.0 %all-to-all-start.2 = ((f32[128,8,128]{2,1,0:T(8,128)}), f32[128,8,128]{2,1,0:T(8,128)}, u32[]{:S(2)}, u32[]{:S(2)}) async-start(f32[128,8,128]{2,1,0:T(8,128)} %fusion.2), calls=%async_computation.2 | async-start | bytes 1048576 | tf_op jit(solution)/shard_map/all_to_all | solution.py:75
  33.9 1.4 scatter_custom_fusion.1
  36.9 4.7 %fusion.10 = f32[256,8,128]{2,1,0:T(8,128)S(1)} fusion(bf16[256,128,128]{2,1,0:T(8,128)(2,1)} %param.29, bf16[256,8,128]{2,1,0:T(8,128)(2,1)S(1)} %gather_fusion, pred[256]{0:T(512)(128)(4,1)S(1)} %compare_and_fusion.3), kind=kOutput, calls=%fused_computation.41 | convolution fusion | flops 67371008 | bytes 9961728 | tf_op jit(solution)/shard_map/rnp,npq->nrq/dot_general | solution.py:47
  41.8 7.0 %scatter_fusion = f32[512,8,128]{2,1,0:T(8,128)S(1)} fusion(f32[512,8,128]{2,1,0:T(8,128)S(1)} %broadcast.333.clone, s32[256]{0:T(256)S(1)} %bitcast.177, f32[256,8,128]{2,1,0:T(8,128)S(1)} %fusion.10), kind=kCustom, calls=%fused_computation.10 | custom fusion | bytes 3146752 | tf_op jit(solution)/shard_map/scatter | solution.py:53
  48.9 1.2 convert_element_type.72
  51.1 9.8 %all-to-all-start.1 = ((bf16[128,4,1]{1,2,0:T(2,128)(2,1)}), bf16[128,4,1]{1,2,0:T(2,128)(2,1)S(1)}, u32[]{:S(2)}, u32[]{:S(2)}) async-start(bf16[128,4,1]{1,2,0:T(2,128)(2,1)} %all_to_all.33), calls=%async_computation.1 | async-start | bytes 131072 | tf_op jit(solution)/shard_map/all_to_all | solution.py:63
  61.9 10.6 %all_gather.12 = bf16[128,8,128]{2,1,0:T(8,128)(2,1)S(1)} all-gather(bf16[32,8,128]{2,1,0:T(8,128)(2,1)S(1)} %bitcast_reduce_fusion.1), channel_id=1, replica_groups=mesh['leaf'=32,'level'=4] {'level'}, dimensions={0}, use_global_device_ids=true | all-gather | bytes 327680 | tf_op jit(solution)/shard_map/all_gather | solution.py:98
  73.4 2.8 %fusion.4 = bf16[32,8,128]{2,1,0:T(8,128)(2,1)S(1)} fusion(bf16[32,4,8,128]{3,2,1,0:T(8,128)(2,1)S(1)} %bitcast.169, bf16[32,4,128,128]{3,2,1,0:T(8,128)(2,1)} %param.25), kind=kOutput, calls=%fused_computation.30 | convolution fusion | flops 33587200 | bytes 4521984 | tf_op jit(solution)/shard_map/qfrk,qfkj->qrj/dot_general | solution.py:102
  77.0 11.4 %all-to-all-start.3 = ((bf16[128,8,128]{2,1,0:T(8,128)(2,1)}), bf16[128,8,128]{2,1,0:T(8,128)(2,1)S(1)}, u32[]{:S(2)}, u32[]{:S(2)}) async-start(bf16[128,8,128]{2,1,0:T(8,128)(2,1)} %bitcast.20), calls=%async_computation.3 | async-start | bytes 524288 | tf_op jit(solution)/shard_map/all_to_all | solution.py:79
  88.5 11.3 %all-to-all-done.3 = bf16[128,8,128]{2,1,0:T(8,128)(2,1)S(1)} async-done(((bf16[128,8,128]{2,1,0:T(8,128)(2,1)}), bf16[128,8,128]{2,1,0:T(8,128)(2,1)S(1)}, u32[]{:S(2)}, u32[]{:S(2)}) %all-to-all-start.3) | async-done | bytes 262176 | tf_op jit(solution)/shard_map/all_to_all | solution.py:79
  99.8 3.9 %all-to-all-start = ((bf16[512,8,128]{2,1,0:T(8,128)(2,1)}), bf16[512,8,128]{2,1,0:T(8,128)(2,1)S(1)}, u32[]{:S(2)}, u32[]{:S(2)}) async-start(bf16[512,8,128]{2,1,0:T(8,128)(2,1)} %convert_element_type.72), calls=%async_computation | async-start | bytes 2097152 | tf_op jit(solution)/shard_map/all_to_all | solution.py:56
  104.0 6.9 %convolution_bitcast_fusion.1 = f32[8,128,128]{2,0,1:T(8,128)S(1)} fusion(bf16[128,8,128]{2,1,0:T(8,128)(2,1)S(1)} %all-to-all-done.3, bf16[128,128,128]{2,1,0:T(8,128)(2,1)} %gather_fusion.1, pred[128]{0:T(512)(128)(4,1)S(1)} %compare_and_fusion.2, bf16[128,128,128]{2,1,0:T(8,128)(2,1)} %gather_fusion.3), kind=kOutput, calls=%fused_computation.17 | convolution fusion | flops 71434240 | bytes 9175168 | tf_op jit(solution)/shard_map/srk,spk->rsp/dot_general | solution.py:109
  111.9 11.5 %all-to-all-done = bf16[512,8,128]{2,1,0:T(8,128)(2,1)S(1)} async-done(((bf16[512,8,128]{2,1,0:T(8,128)(2,1)}), bf16[512,8,128]{2,1,0:T(8,128)(2,1)S(1)}, u32[]{:S(2)}, u32[]{:S(2)}) %all-to-all-start) | async-done | bytes 1048608 | tf_op jit(solution)/shard_map/all_to_all | solution.py:56
  123.4 1.4 multiply_convert_fusion
  125.6 6.6 %fusion.3 = f32[128,8,128]{2,1,0:T(8,128)} fusion(bf16[128,8,128]{2,1,0:T(8,128)(2,1)S(1)} %gather_fusion.7, pred[128]{0:T(512)(128)(4,1)S(1)} %compare_and_fusion.2, bf16[128,128,128]{2,1,0:T(8,128)(2,1)} %gather_fusion.1, bf16[128,128,128]{2,1,0:T(8,128)(2,1)} %gather_fusion.3), kind=kOutput, calls=%fused_computation.27 | convolution fusion | flops 71565312 | bytes 9175168 | tf_op jit(solution)/shard_map/srk,skj->srj/dot_general | solution.py:91
  132.2 3.7 %all-to-all-start.5 = ((f32[128,8,128]{2,1,0:T(8,128)}), f32[128,8,128]{2,1,0:T(8,128)S(1)}, u32[]{:S(2)}, u32[]{:S(2)}) async-start(f32[128,8,128]{2,1,0:T(8,128)} %fusion.3), calls=%async_computation.5 | async-start | bytes 1048576 | tf_op jit(solution)/shard_map/all_to_all | solution.py:75
  136.7 13.5 %all-to-all-done.5 = f32[128,8,128]{2,1,0:T(8,128)S(1)} async-done(((f32[128,8,128]{2,1,0:T(8,128)}), f32[128,8,128]{2,1,0:T(8,128)S(1)}, u32[]{:S(2)}, u32[]{:S(2)}) %all-to-all-start.5) | async-done | bytes 524320 | tf_op jit(solution)/shard_map/all_to_all | solution.py:75
  150.2 9.4 %all_gather.13 = bf16[128,8,128]{2,1,0:T(8,128)(2,1)S(1)} all-gather(bf16[32,8,128]{2,1,0:T(8,128)(2,1)S(1)} %bitcast_reduce_fusion), channel_id=1, replica_groups=mesh['leaf'=32,'level'=4] {'level'}, dimensions={0}, use_global_device_ids=true | all-gather | bytes 327680 | tf_op jit(solution)/shard_map/all_gather | solution.py:98
  160.5 2.8 %fusion.5 = bf16[32,8,128]{2,1,0:T(8,128)(2,1)S(1)} fusion(bf16[32,4,8,128]{3,2,1,0:T(8,128)(2,1)S(1)} %bitcast.168, bf16[32,4,128,128]{3,2,1,0:T(8,128)(2,1)} %param.25), kind=kOutput, calls=%fused_computation.31 | convolution fusion | flops 33587200 | bytes 4521984 | tf_op jit(solution)/shard_map/qfrk,qfkj->qrj/dot_general | solution.py:102
  164.1 7.6 %all-to-all-start.6 = ((bf16[128,8,128]{2,1,0:T(8,128)(2,1)}), bf16[128,8,128]{2,1,0:T(8,128)(2,1)S(1)}, u32[]{:S(2)}, u32[]{:S(2)}) async-start(bf16[128,8,128]{2,1,0:T(8,128)(2,1)} %bitcast.32), calls=%async_computation.6 | async-start | bytes 524288 | tf_op jit(solution)/shard_map/all_to_all | solution.py:79
  171.7 4.7 %fusion.8 = f32[256,8,128]{2,1,0:T(8,128)S(1)} fusion(bf16[256,128,128]{2,1,0:T(8,128)(2,1)} %param.29, bf16[256,8,128]{2,1,0:T(8,128)(2,1)S(1)} %gather_fusion.6, pred[256]{0:T(512)(128)(4,1)S(1)} %compare_and_fusion.3), kind=kOutput, calls=%fused_computation.38 | convolution fusion | flops 67371008 | bytes 9961728 | tf_op jit(solution)/shard_map/rnp,npq->nrq/dot_general | solution.py:47
  176.6 7.0 %scatter_fusion.1 = f32[512,8,128]{2,1,0:T(8,128)S(1)} fusion(f32[512,8,128]{2,1,0:T(8,128)S(1)} %broadcast.333, s32[256]{0:T(256)S(1)} %bitcast.178, f32[256,8,128]{2,1,0:T(8,128)S(1)} %fusion.8), kind=kCustom, calls=%fused_computation.13 | custom fusion | bytes 3146752 | tf_op jit(solution)/shard_map/scatter | solution.py:53
  184.7 10.2 %all-to-all-start.4 = ((bf16[512,8,128]{2,1,0:T(8,128)(2,1)}), bf16[512,8,128]{2,1,0:T(8,128)(2,1)}, u32[]{:S(2)}, u32[]{:S(2)}) async-start(bf16[512,8,128]{2,1,0:T(8,128)(2,1)} %convert_element_type.83), calls=%async_computation.4 | async-start | bytes 2097152 | tf_op jit(solution)/shard_map/all_to_all | solution.py:56
  195.3 7.0 %convolution_bitcast_fusion = f32[8,128,128]{2,0,1:T(8,128)S(1)} fusion(bf16[128,8,128]{2,1,0:T(8,128)(2,1)S(1)} %all-to-all-done.6, bf16[128,128,128]{2,1,0:T(8,128)(2,1)} %gather_fusion.1, pred[128]{0:T(512)(128)(4,1)S(1)} %compare_and_fusion.2, bf16[128,128,128]{2,1,0:T(8,128)(2,1)} %gather_fusion.3), kind=kOutput, calls=%fused_computation.16 | convolution fusion | flops 71434240 | bytes 9175168 | tf_op jit(solution)/shard_map/srk,spk->rsp/dot_general | solution.py:109
  203.3 11.0 %all-to-all-done.4 = bf16[512,8,128]{2,1,0:T(8,128)(2,1)} async-done(((bf16[512,8,128]{2,1,0:T(8,128)(2,1)}), bf16[512,8,128]{2,1,0:T(8,128)(2,1)}, u32[]{:S(2)}, u32[]{:S(2)}) %all-to-all-start.4) | async-done | bytes 1048608 | tf_op jit(solution)/shard_map/all_to_all | solution.py:56
  214.3 1.9 multiply_reduce_fusion
  216.3 53.0 %all-gather.1 = f32[128,6,8]{2,1,0:T(8,128)S(1)} all-gather(f32[1,6,8]{2,1,0:T(8,128)S(1)} %bitcast.172), channel_id=2, replica_groups=mesh['leaf'=32,'level'=4] {'leaf','level'}, dimensions={0}, use_global_device_ids=true | all-gather | bytes 24768 | tf_op jit(solution)/shard_map/all_gather | solution.py:132
  270.2 1.6 copy_bitcast_fusion
  (81 shorter events, 16.4 us)
Async XLA Ops:
  14.4 18.6 %copy-start.6 = (s32[1,128]{1,0:T(1,128)S(1)}, s32[1,128]{1,0:T(1,128)}, u32[]{:S(2)}) copy-start(s32[1,128]{1,0:T(1,128)} %param.23) | copy-start | bytes 1540
  14.4 18.7 %copy-start.4 = (s32[256]{0:T(256)S(1)}, s32[256]{0:T(256)}, u32[]{:S(2)}) copy-start(s32[256]{0:T(256)} %param.26) | copy-start | bytes 3076
  14.4 18.7 %copy-start.5 = (s32[256]{0:T(256)S(1)}, s32[256]{0:T(256)}, u32[]{:S(2)}) copy-start(s32[256]{0:T(256)} %param.28) | copy-start | bytes 3076
  14.4 18.7 %copy-start.3 = (s32[32,4]{0,1:T(4,128)S(1)}, s32[32,4]{0,1:T(4,128)}, u32[]{:S(2)}) copy-start(s32[32,4]{0,1:T(4,128)} %param.24) | copy-start | bytes 1540
  14.4 18.9 %copy-start.2 = (s32[256,1]{0,1:T(1,128)S(1)}, s32[256,1]{0,1:T(1,128)}, u32[]{:S(2)}) copy-start(s32[256,1]{0,1:T(1,128)} %param.27) | copy-start | bytes 3076
  21.1 30.0 %all-to-all-start.2 = ((f32[128,8,128]{2,1,0:T(8,128)}), f32[128,8,128]{2,1,0:T(8,128)}, u32[]{:S(2)}, u32[]{:S(2)}) async-start(f32[128,8,128]{2,1,0:T(8,128)} %fusion.2), calls=%async_computation.2 | async-start | bytes 1048576 | tf_op jit(solution)/shard_map/all_to_all | solution.py:75
  51.1 25.2 %all-to-all-start.1 = ((bf16[128,4,1]{1,2,0:T(2,128)(2,1)}), bf16[128,4,1]{1,2,0:T(2,128)(2,1)S(1)}, u32[]{:S(2)}, u32[]{:S(2)}) async-start(bf16[128,4,1]{1,2,0:T(2,128)(2,1)} %all_to_all.33), calls=%async_computation.1 | async-start | bytes 131072 | tf_op jit(solution)/shard_map/all_to_all | solution.py:63
  77.0 22.7 %all-to-all-start.3 = ((bf16[128,8,128]{2,1,0:T(8,128)(2,1)}), bf16[128,8,128]{2,1,0:T(8,128)(2,1)S(1)}, u32[]{:S(2)}, u32[]{:S(2)}) async-start(bf16[128,8,128]{2,1,0:T(8,128)(2,1)} %bitcast.20), calls=%async_computation.3 | async-start | bytes 524288 | tf_op jit(solution)/shard_map/all_to_all | solution.py:79
  99.8 23.6 %all-to-all-start = ((bf16[512,8,128]{2,1,0:T(8,128)(2,1)}), bf16[512,8,128]{2,1,0:T(8,128)(2,1)S(1)}, u32[]{:S(2)}, u32[]{:S(2)}) async-start(bf16[512,8,128]{2,1,0:T(8,128)(2,1)} %convert_element_type.72), calls=%async_computation | async-start | bytes 2097152 | tf_op jit(solution)/shard_map/all_to_all | solution.py:56
  132.2 17.9 %all-to-all-start.5 = ((f32[128,8,128]{2,1,0:T(8,128)}), f32[128,8,128]{2,1,0:T(8,128)S(1)}, u32[]{:S(2)}, u32[]{:S(2)}) async-start(f32[128,8,128]{2,1,0:T(8,128)} %fusion.3), calls=%async_computation.5 | async-start | bytes 1048576 | tf_op jit(solution)/shard_map/all_to_all | solution.py:75
  164.1 20.6 %all-to-all-start.6 = ((bf16[128,8,128]{2,1,0:T(8,128)(2,1)}), bf16[128,8,128]{2,1,0:T(8,128)(2,1)S(1)}, u32[]{:S(2)}, u32[]{:S(2)}) async-start(bf16[128,8,128]{2,1,0:T(8,128)(2,1)} %bitcast.32), calls=%async_computation.6 | async-start | bytes 524288 | tf_op jit(solution)/shard_map/all_to_all | solution.py:79
  183.6 11.3 %copy-start.1 = (f32[8,16384]{1,0:T(8,128)S(1)}, f32[8,16384]{1,0:T(8,128)}, u32[]{:S(2)}) copy-start(f32[8,16384]{1,0:T(8,128)} %param.20) | copy-start | bytes 1572868
  184.7 29.6 %all-to-all-start.4 = ((bf16[512,8,128]{2,1,0:T(8,128)(2,1)}), bf16[512,8,128]{2,1,0:T(8,128)(2,1)}, u32[]{:S(2)}, u32[]{:S(2)}) async-start(bf16[512,8,128]{2,1,0:T(8,128)(2,1)} %convert_element_type.83), calls=%async_computation.4 | async-start | bytes 2097152 | tf_op jit(solution)/shard_map/all_to_all | solution.py:56
  195.3 19.1 %copy-start = (f32[8,128,128]{1,2,0:T(8,128)S(1)}, f32[8,128,128]{1,2,0:T(8,128)}, u32[]{:S(2)}) copy-start(f32[8,128,128]{1,2,0:T(8,128)} %get-tuple-element.34) | copy-start | bytes 1572868
where the time goes:
time: 273 us; the launch traced here: 272 us
  blocking collectives  73 us (27%)
  starting transfers between devices  58.5 us (21%)
  waiting for transfers between devices  47.3 us (17%)
  matrix products  45.6 us (17%)
  local copies, waits for them, and re-layouts  38.8 us (14%)
  other arithmetic  7.56 us (3%)
    all_gather x1, blocking collectives, local(): dots = jnp.sum(lax.all_gather(own, ('leaf', 'level')), axis=0)  53 us
    all_to_all x2, waiting for transfers between devices, near_field(): lax.all_to_all(outgoing.astype(jnp.bfloat16), ('leaf', 'level'), split_ax...  22.5 us
    all_gather x2, blocking collectives, operator(): parent_table = lax.all_gather(parent_rows, 'level', axis=0, tiled=True)  20 us
    all_to_all x2, starting transfers between devices, downward(): lax.all_to_all(spread, ('leaf', 'level'), split_axis=0, concat_axis=0, ti...  19 us
    all_to_all x2, starting transfers between devices, upward(): lax.all_to_all(lifted, ('leaf', 'level'), split_axis=0, concat_axis=0, ti...  15.6 us
    all_to_all x2, starting transfers between devices, near_field(): lax.all_to_all(outgoing.astype(jnp.bfloat16), ('leaf', 'level'), split_ax...  14.1 us
    scatter x2, local copies, waits for them, and re-layouts, near_field(): outgoing = jnp.zeros((groups * capacity, systems, points), jnp.float32).a...  14.1 us
    dot_general x2, matrix products, operator(): jnp.einsum('srk,spk->rsp', expanded, basis_slot, preferred_element_type=j...  13.9 us
  transfers between devices with their start and end apart: 7, of which 4 were waited for; matrix products, arithmetic and copies ran while one was open for 19% of the time, Pallas kernels for 0%

commit v1 on v0

--- a/solution.py
+++ b/solution.py
@@ -6,6 +6,12 @@
 CHILDREN = 4
 EPSILON = 1e-06
 SCALE = 2.0 ** (-20)
+
+
+def _define_side(vals, mesh_name):
+    row_out = jnp.stack([vals for _ in range(lax.axis_size(mesh_name))])
+    o_now = lax.all_to_all(row_out, axis_name=mesh_name, split_axis=0, concat_axis=0)
+    return jnp.concatenate(o_now, axis=0)
 
 
 def local(
@@ -95,7 +101,7 @@
         parent_rows = jnp.sum(arrived.reshape(parents, CHILDREN, systems, coeffs), axis=1).astype(
             jnp.bfloat16
         )
-        parent_table = lax.all_gather(parent_rows, "level", axis=0, tiled=True)
+        parent_table = _define_side(parent_rows, "level")
         picked = jnp.take(parent_table, far_src.reshape(-1), axis=0).reshape(
             parents, partners, systems, coeffs
         )

time: 273 us -> 267 us (0.978)
  starting transfers between devices: 58.5 us -> 51.4 us
  waiting for transfers between devices: 47.3 us -> 51.4 us
    all_gather x2 -> x0, blocking collectives: 20 us -> none  [operator(): parent_table = lax.all_gather(parent_rows, 'level', axis=0, tiled=True)]
    all_to_all x0 -> x1, blocking collectives: none -> 17.4 us  [upward(): lax.all_to_all(lifted, ('leaf', 'level'), split_axis=0, concat_axis=0, ti...]
    all_to_all x2 -> x1, waiting for transfers between devices: 13.5 us -> 0.01 us  [upward(): lax.all_to_all(lifted, ('leaf', 'level'), split_axis=0, concat_axis=0, ti...]
    all_to_all x0 -> x2, waiting for transfers between devices: none -> 11.5 us  [_define_side(): lax.all_to_all(row_out, axis_name=mesh_name, split_axis=0, concat_axis=0)]
    all_to_all x2, starting transfers between devices: 19 us -> 8.43 us  [downward(): lax.all_to_all(spread, ('leaf', 'level'), split_axis=0, concat_axis=0, ti...]
    all_to_all x0 -> x2, starting transfers between devices: none -> 7.57 us  [_define_side(): lax.all_to_all(row_out, axis_name=mesh_name, split_axis=0, concat_axis=0)]
    all_to_all x1, waiting for transfers between devices: 0.01 us -> 6.07 us  [near_field(): lax.all_to_all(source_label.astype(jnp.bfloat16), ('leaf', 'level'), spli...]
    all_to_all x2 -> x1, starting transfers between devices: 15.6 us -> 12 us  [upward(): lax.all_to_all(lifted, ('leaf', 'level'), split_axis=0, concat_axis=0, ti...]
  transfers between devices with their start and end apart: 7 -> 8, of which waited for: 4 -> 6; matrix products, arithmetic and copies ran while one was open for 19% -> 19% of each run, Pallas kernels for 0% -> 0%
where the time goes in v1:
time: 267 us; the launch traced here: 266 us
  blocking collectives  70.3 us (26%)
  starting transfers between devices  51.4 us (19%)
  waiting for transfers between devices  51.4 us (19%)
  matrix products  43.8 us (16%)
  local copies, waits for them, and re-layouts  40.2 us (15%)
  other arithmetic  7.55 us (3%)
    all_gather x1, blocking collectives, local(): dots = jnp.sum(lax.all_gather(own, ('leaf', 'level')), axis=0)  53 us
    all_to_all x2, waiting for transfers between devices, near_field(): lax.all_to_all(outgoing.astype(jnp.bfloat16), ('leaf', 'level'), split_ax...  22.5 us
    all_to_all x1, blocking collectives, upward(): lax.all_to_all(lifted, ('leaf', 'level'), split_axis=0, concat_axis=0, ti...  17.4 us
    all_to_all x2, starting transfers between devices, near_field(): lax.all_to_all(outgoing.astype(jnp.bfloat16), ('leaf', 'level'), split_ax...  14.2 us
    scatter x2, local copies, waits for them, and re-layouts, near_field(): outgoing = jnp.zeros((groups * capacity, systems, points), jnp.float32).a...  14.1 us
    dot_general x2, matrix products, operator(): jnp.einsum('srk,spk->rsp', expanded, basis_slot, preferred_element_type=j...  13.9 us
    all_to_all x1, starting transfers between devices, upward(): lax.all_to_all(lifted, ('leaf', 'level'), split_axis=0, concat_axis=0, ti...  12 us
    all_to_all x2, waiting for transfers between devices, _define_side(): lax.all_to_all(row_out, axis_name=mesh_name, split_axis=0, concat_axis=0)  11.5 us
  transfers between devices with their start and end apart: 8, of which 6 were waited for; matrix products, arithmetic and copies ran while one was open for 19% of the time, Pallas kernels for 0%

profile of v1, /device:TPU:1, one launch (start us, length us, event | category | flops | bytes accessed | tf_op | source)
XLA Modules:
  0.0 265.8 jit_solution(9308878808702137166)
XLA Ops:
  3.9 5.2 %gather_fusion.3 = bf16[128,128,128]{2,1,0:T(8,128)(2,1)} fusion(bf16[128,128,128]{2,1,0:T(8,128)(2,1)} %param.22, s32[1024]{0:T(1024)S(1)} %pad_clamp_fusion.2), kind=kCustom, calls=%fused_computation.6.clone | custom fusion | bytes 8389120 | tf_op jit(solution)/shard_map/jit(_take)/gather | solution.py:39
  9.2 5.2 %gather_fusion.1 = bf16[128,128,128]{2,1,0:T(8,128)(2,1)} fusion(bf16[128,128,128]{2,1,0:T(8,128)(2,1)} %param.21, s32[1024]{0:T(1024)S(1)} %pad_clamp_fusion.2), kind=kCustom, calls=%fused_computation.1.clone | custom fusion | bytes 8389120 | tf_op jit(solution)/shard_map/jit(_take)/gather | solution.py:38
  14.4 6.7 %fusion.2 = f32[128,8,128]{2,1,0:T(8,128)} fusion(bf16[128,8,128]{2,1,0:T(8,128)(2,1)S(1)} %gather_fusion.2, pred[128]{0:T(512)(128)(4,1)S(1)} %compare_and_fusion.2, bf16[128,128,128]{2,1,0:T(8,128)(2,1)} %gather_fusion.1, bf16[128,128,128]{2,1,0:T(8,128)(2,1)} %gather_fusion.3), kind=kOutput, calls=%fused_computation.26 | convolution fusion | flops 71565312 | bytes 9175168 | tf_op jit(solution)/shard_map/srk,skj->srj/dot_general | solution.py:97
  21.0 12.0 %all-to-all-start.2 = ((f32[128,8,128]{2,1,0:T(8,128)}), f32[128,8,128]{2,1,0:T(8,128)}, u32[]{:S(2)}, u32[]{:S(2)}) async-start(f32[128,8,128]{2,1,0:T(8,128)} %fusion.2), calls=%async_computation.2 | async-start | bytes 1048576 | tf_op jit(solution)/shard_map/all_to_all | solution.py:81
  33.9 1.4 scatter_custom_fusion.1
  36.9 4.7 %fusion.10 = f32[256,8,128]{2,1,0:T(8,128)S(1)} fusion(bf16[256,128,128]{2,1,0:T(8,128)(2,1)} %param.29, bf16[256,8,128]{2,1,0:T(8,128)(2,1)S(1)} %gather_fusion, pred[256]{0:T(512)(128)(4,1)S(1)} %compare_and_fusion.3), kind=kOutput, calls=%fused_computation.41 | convolution fusion | flops 67371008 | bytes 9961728 | tf_op jit(solution)/shard_map/rnp,npq->nrq/dot_general | solution.py:53
  41.8 7.0 %scatter_fusion = f32[512,8,128]{2,1,0:T(8,128)S(1)} fusion(f32[512,8,128]{2,1,0:T(8,128)S(1)} %broadcast.335.clone, s32[256]{0:T(256)S(1)} %bitcast.181, f32[256,8,128]{2,1,0:T(8,128)S(1)} %fusion.10), kind=kCustom, calls=%fused_computation.10 | custom fusion | bytes 3146752 | tf_op jit(solution)/shard_map/scatter | solution.py:59
  52.9 4.2 %all-to-all-start.3 = ((bf16[4,32,8,128]{3,2,1,0:T(8,128)(2,1)}), bf16[4,32,8,128]{3,2,1,0:T(8,128)(2,1)S(1)}, u32[]{:S(2)}, u32[]{:S(2)}) async-start(bf16[4,32,8,128]{3,2,1,0:T(8,128)(2,1)} %stack.36), calls=%async_computation.3 | async-start | bytes 524288 | tf_op jit(solution)/shard_map/all_to_all | solution.py:13
  57.0 5.8 %all-to-all-done.3 = bf16[4,32,8,128]{3,2,1,0:T(8,128)(2,1)S(1)} async-done(((bf16[4,32,8,128]{3,2,1,0:T(8,128)(2,1)}), bf16[4,32,8,128]{3,2,1,0:T(8,128)(2,1)S(1)}, u32[]{:S(2)}, u32[]{:S(2)}) %all-to-all-start.3) | async-done | bytes 262176 | tf_op jit(solution)/shard_map/all_to_all | solution.py:13
  62.8 9.2 %all-to-all-start.1 = ((bf16[128,4,1]{1,2,0:T(2,128)(2,1)}), bf16[128,4,1]{1,2,0:T(2,128)(2,1)S(1)}, u32[]{:S(2)}, u32[]{:S(2)}) async-start(bf16[128,4,1]{1,2,0:T(2,128)(2,1)} %all_to_all.41), calls=%async_computation.1 | async-start | bytes 131072 | tf_op jit(solution)/shard_map/all_to_all | solution.py:69
  72.9 2.8 %fusion.4 = bf16[32,8,128]{2,1,0:T(8,128)(2,1)S(1)} fusion(bf16[32,4,8,128]{3,2,1,0:T(8,128)(2,1)S(1)} %bitcast.171, bf16[32,4,128,128]{3,2,1,0:T(8,128)(2,1)} %param.25), kind=kOutput, calls=%fused_computation.30 | convolution fusion | flops 33587200 | bytes 4521984 | tf_op jit(solution)/shard_map/qfrk,qfkj->qrj/dot_general | solution.py:108
  75.8 6.1 %all-to-all-done.1 = bf16[128,4,1]{1,2,0:T(2,128)(2,1)S(1)} async-done(((bf16[128,4,1]{1,2,0:T(2,128)(2,1)}), bf16[128,4,1]{1,2,0:T(2,128)(2,1)S(1)}, u32[]{:S(2)}, u32[]{:S(2)}) %all-to-all-start.1) | async-done | bytes 1056 | tf_op jit(solution)/shard_map/all_to_all | solution.py:69
  82.6 4.0 %all-to-all-start.4 = ((bf16[128,8,128]{2,1,0:T(8,128)(2,1)}), bf16[128,8,128]{2,1,0:T(8,128)(2,1)S(1)}, u32[]{:S(2)}, u32[]{:S(2)}) async-start(bf16[128,8,128]{2,1,0:T(8,128)(2,1)} %bitcast.21), calls=%async_computation.4 | async-start | bytes 524288 | tf_op jit(solution)/shard_map/all_to_all | solution.py:85
  86.6 11.3 %all-to-all-done.4 = bf16[128,8,128]{2,1,0:T(8,128)(2,1)S(1)} async-done(((bf16[128,8,128]{2,1,0:T(8,128)(2,1)}), bf16[128,8,128]{2,1,0:T(8,128)(2,1)S(1)}, u32[]{:S(2)}, u32[]{:S(2)}) %all-to-all-start.4) | async-done | bytes 262176 | tf_op jit(solution)/shard_map/all_to_all | solution.py:85
  97.9 3.9 %all-to-all-start = ((bf16[512,8,128]{2,1,0:T(8,128)(2,1)}), bf16[512,8,128]{2,1,0:T(8,128)(2,1)S(1)}, u32[]{:S(2)}, u32[]{:S(2)}) async-start(bf16[512,8,128]{2,1,0:T(8,128)(2,1)} %convert_element_type.76), calls=%async_computation | async-start | bytes 2097152 | tf_op jit(solution)/shard_map/all_to_all | solution.py:62
  102.1 6.9 %convolution_bitcast_fusion.1 = f32[8,128,128]{2,0,1:T(8,128)S(1)} fusion(bf16[128,8,128]{2,1,0:T(8,128)(2,1)S(1)} %all-to-all-done.4, bf16[128,128,128]{2,1,0:T(8,128)(2,1)} %gather_fusion.1, pred[128]{0:T(512)(128)(4,1)S(1)} %compare_and_fusion.2, bf16[128,128,128]{2,1,0:T(8,128)(2,1)} %gather_fusion.3), kind=kOutput, calls=%fused_computation.17 | convolution fusion | flops 71434240 | bytes 9175168 | tf_op jit(solution)/shard_map/srk,spk->rsp/dot_general | solution.py:115
  110.0 11.5 %all-to-all-done = bf16[512,8,128]{2,1,0:T(8,128)(2,1)S(1)} async-done(((bf16[512,8,128]{2,1,0:T(8,128)(2,1)}), bf16[512,8,128]{2,1,0:T(8,128)(2,1)S(1)}, u32[]{:S(2)}, u32[]{:S(2)}) %all-to-all-start) | async-done | bytes 1048608 | tf_op jit(solution)/shard_map/all_to_all | solution.py:62
  121.5 1.3 multiply_convert_fusion
  123.8 4.8 %fusion.3 = f32[128,8,128]{2,1,0:T(8,128)S(1)} fusion(bf16[128,8,128]{2,1,0:T(8,128)(2,1)S(1)} %gather_fusion.7, pred[128]{0:T(512)(128)(4,1)S(1)} %compare_and_fusion.2, bf16[128,128,128]{2,1,0:T(8,128)(2,1)} %gather_fusion.1, bf16[128,128,128]{2,1,0:T(8,128)(2,1)} %gather_fusion.3), kind=kOutput, calls=%fused_computation.27 | convolution fusion | flops 71565312 | bytes 9175168 | tf_op jit(solution)/shard_map/srk,skj->srj/dot_general | solution.py:97
  128.5 17.4 %all_to_all.51 = f32[128,8,128]{2,1,0:T(8,128)S(1)} all-to-all(f32[128,8,128]{2,1,0:T(8,128)S(1)} %fusion.3), channel_id=1, replica_groups=mesh['leaf'=32,'level'=4] {'leaf','level'}, dimensions={0} | all-to-all | bytes 1048576 | tf_op jit(solution)/shard_map/all_to_all | solution.py:81
  146.7 3.4 %all-to-all-start.7 = ((bf16[4,32,8,128]{3,2,1,0:T(8,128)(2,1)}), bf16[4,32,8,128]{3,2,1,0:T(8,128)(2,1)S(1)}, u32[]{:S(2)}, u32[]{:S(2)}) async-start(bf16[4,32,8,128]{3,2,1,0:T(8,128)(2,1)} %stack.39), calls=%async_computation.7 | async-start | bytes 524288 | tf_op jit(solution)/shard_map/all_to_all | solution.py:13
  150.9 5.7 %all-to-all-done.7 = bf16[4,32,8,128]{3,2,1,0:T(8,128)(2,1)S(1)} async-done(((bf16[4,32,8,128]{3,2,1,0:T(8,128)(2,1)}), bf16[4,32,8,128]{3,2,1,0:T(8,128)(2,1)S(1)}, u32[]{:S(2)}, u32[]{:S(2)}) %all-to-all-start.7) | async-done | bytes 262176 | tf_op jit(solution)/shard_map/all_to_all | solution.py:13
  157.5 2.8 %fusion.5 = bf16[32,8,128]{2,1,0:T(8,128)(2,1)S(1)} fusion(bf16[32,4,8,128]{3,2,1,0:T(8,128)(2,1)S(1)} %bitcast.170, bf16[32,4,128,128]{3,2,1,0:T(8,128)(2,1)} %param.25), kind=kOutput, calls=%fused_computation.31 | convolution fusion | flops 33587200 | bytes 4521984 | tf_op jit(solution)/shard_map/qfrk,qfkj->qrj/dot_general | solution.py:108
  161.1 4.5 %all-to-all-start.8 = ((bf16[128,8,128]{2,1,0:T(8,128)(2,1)}), bf16[128,8,128]{2,1,0:T(8,128)(2,1)S(1)}, u32[]{:S(2)}, u32[]{:S(2)}) async-start(bf16[128,8,128]{2,1,0:T(8,128)(2,1)} %bitcast.34), calls=%async_computation.8 | async-start | bytes 524288 | tf_op jit(solution)/shard_map/all_to_all | solution.py:85
  165.6 4.7 %fusion.8 = f32[256,8,128]{2,1,0:T(8,128)S(1)} fusion(bf16[256,128,128]{2,1,0:T(8,128)(2,1)} %param.29, bf16[256,8,128]{2,1,0:T(8,128)(2,1)S(1)} %gather_fusion.6, pred[256]{0:T(512)(128)(4,1)S(1)} %compare_and_fusion.3), kind=kOutput, calls=%fused_computation.38 | convolution fusion | flops 67371008 | bytes 9961728 | tf_op jit(solution)/shard_map/rnp,npq->nrq/dot_general | solution.py:53
  170.5 7.0 %scatter_fusion.1 = f32[512,8,128]{2,1,0:T(8,128)S(1)} fusion(f32[512,8,128]{2,1,0:T(8,128)S(1)} %broadcast.335, s32[256]{0:T(256)S(1)} %bitcast.182, f32[256,8,128]{2,1,0:T(8,128)S(1)} %fusion.8), kind=kCustom, calls=%fused_computation.13 | custom fusion | bytes 3146752 | tf_op jit(solution)/shard_map/scatter | solution.py:59
  178.6 10.4 %all-to-all-start.5 = ((bf16[512,8,128]{2,1,0:T(8,128)(2,1)}), bf16[512,8,128]{2,1,0:T(8,128)(2,1)}, u32[]{:S(2)}, u32[]{:S(2)}) async-start(bf16[512,8,128]{2,1,0:T(8,128)(2,1)} %convert_element_type.87), calls=%async_computation.5 | async-start | bytes 2097152 | tf_op jit(solution)/shard_map/all_to_all | solution.py:62
  189.3 7.0 %convolution_bitcast_fusion = f32[8,128,128]{2,0,1:T(8,128)S(1)} fusion(bf16[128,8,128]{2,1,0:T(8,128)(2,1)S(1)} %all-to-all-done.8, bf16[128,128,128]{2,1,0:T(8,128)(2,1)} %gather_fusion.1, pred[128]{0:T(512)(128)(4,1)S(1)} %compare_and_fusion.2, bf16[128,128,128]{2,1,0:T(8,128)(2,1)} %gather_fusion.3), kind=kOutput, calls=%fused_computation.16 | convolution fusion | flops 71434240 | bytes 9175168 | tf_op jit(solution)/shard_map/srk,spk->rsp/dot_general | solution.py:115
  197.3 11.0 %all-to-all-done.5 = bf16[512,8,128]{2,1,0:T(8,128)(2,1)} async-done(((bf16[512,8,128]{2,1,0:T(8,128)(2,1)}), bf16[512,8,128]{2,1,0:T(8,128)(2,1)}, u32[]{:S(2)}, u32[]{:S(2)}) %all-to-all-start.5) | async-done | bytes 1048608 | tf_op jit(solution)/shard_map/all_to_all | solution.py:62
  208.4 1.9 multiply_reduce_fusion
  210.3 53.0 %all-gather.1 = f32[128,6,8]{2,1,0:T(8,128)S(1)} all-gather(f32[1,6,8]{2,1,0:T(8,128)S(1)} %bitcast.176), channel_id=2, replica_groups=mesh['leaf'=32,'level'=4] {'leaf','level'}, dimensions={0}, use_global_device_ids=true | all-gather | bytes 24768 | tf_op jit(solution)/shard_map/all_gather | solution.py:138
  264.2 1.6 copy_bitcast_fusion
  (84 shorter events, 20.3 us)
Async XLA Ops:
  14.4 18.6 %copy-start.4 = (s32[256]{0:T(256)S(1)}, s32[256]{0:T(256)}, u32[]{:S(2)}) copy-start(s32[256]{0:T(256)} %param.26) | copy-start | bytes 3076
  14.4 18.7 %copy-start.5 = (s32[256]{0:T(256)S(1)}, s32[256]{0:T(256)}, u32[]{:S(2)}) copy-start(s32[256]{0:T(256)} %param.28) | copy-start | bytes 3076
  14.4 18.7 %copy-start.3 = (s32[32,4]{0,1:T(4,128)S(1)}, s32[32,4]{0,1:T(4,128)}, u32[]{:S(2)}) copy-start(s32[32,4]{0,1:T(4,128)} %param.24) | copy-start | bytes 1540
  14.4 18.9 %copy-start.2 = (s32[256,1]{0,1:T(1,128)S(1)}, s32[256,1]{0,1:T(1,128)}, u32[]{:S(2)}) copy-start(s32[256,1]{0,1:T(1,128)} %param.27) | copy-start | bytes 3076
  21.0 30.0 %all-to-all-start.2 = ((f32[128,8,128]{2,1,0:T(8,128)}), f32[128,8,128]{2,1,0:T(8,128)}, u32[]{:S(2)}, u32[]{:S(2)}) async-start(f32[128,8,128]{2,1,0:T(8,128)} %fusion.2), calls=%async_computation.2 | async-start | bytes 1048576 | tf_op jit(solution)/shard_map/all_to_all | solution.py:81
  41.6 8.4 %copy-start.6 = (s32[1,128]{1,0:T(1,128)S(1)}, s32[1,128]{1,0:T(1,128)}, u32[]{:S(2)}) copy-start(s32[1,128]{1,0:T(1,128)} %param.23) | copy-start | bytes 1540
  52.9 10.0 %all-to-all-start.3 = ((bf16[4,32,8,128]{3,2,1,0:T(8,128)(2,1)}), bf16[4,32,8,128]{3,2,1,0:T(8,128)(2,1)S(1)}, u32[]{:S(2)}, u32[]{:S(2)}) async-start(bf16[4,32,8,128]{3,2,1,0:T(8,128)(2,1)} %stack.36), calls=%async_computation.3 | async-start | bytes 524288 | tf_op jit(solution)/shard_map/all_to_all | solution.py:13
  62.8 19.0 %all-to-all-start.1 = ((bf16[128,4,1]{1,2,0:T(2,128)(2,1)}), bf16[128,4,1]{1,2,0:T(2,128)(2,1)S(1)}, u32[]{:S(2)}, u32[]{:S(2)}) async-start(bf16[128,4,1]{1,2,0:T(2,128)(2,1)} %all_to_all.41), calls=%async_computation.1 | async-start | bytes 131072 | tf_op jit(solution)/shard_map/all_to_all | solution.py:69
  82.6 15.3 %all-to-all-start.4 = ((bf16[128,8,128]{2,1,0:T(8,128)(2,1)}), bf16[128,8,128]{2,1,0:T(8,128)(2,1)S(1)}, u32[]{:S(2)}, u32[]{:S(2)}) async-start(bf16[128,8,128]{2,1,0:T(8,128)(2,1)} %bitcast.21), calls=%async_computation.4 | async-start | bytes 524288 | tf_op jit(solution)/shard_map/all_to_all | solution.py:85
  97.9 23.6 %all-to-all-start = ((bf16[512,8,128]{2,1,0:T(8,128)(2,1)}), bf16[512,8,128]{2,1,0:T(8,128)(2,1)S(1)}, u32[]{:S(2)}, u32[]{:S(2)}) async-start(bf16[512,8,128]{2,1,0:T(8,128)(2,1)} %convert_element_type.76), calls=%async_computation | async-start | bytes 2097152 | tf_op jit(solution)/shard_map/all_to_all | solution.py:62
  146.7 9.9 %all-to-all-start.7 = ((bf16[4,32,8,128]{3,2,1,0:T(8,128)(2,1)}), bf16[4,32,8,128]{3,2,1,0:T(8,128)(2,1)S(1)}, u32[]{:S(2)}, u32[]{:S(2)}) async-start(bf16[4,32,8,128]{3,2,1,0:T(8,128)(2,1)} %stack.39), calls=%async_computation.7 | async-start | bytes 524288 | tf_op jit(solution)/shard_map/all_to_all | solution.py:13
  161.1 17.5 %all-to-all-start.8 = ((bf16[128,8,128]{2,1,0:T(8,128)(2,1)}), bf16[128,8,128]{2,1,0:T(8,128)(2,1)S(1)}, u32[]{:S(2)}, u32[]{:S(2)}) async-start(bf16[128,8,128]{2,1,0:T(8,128)(2,1)} %bitcast.34), calls=%async_computation.8 | async-start | bytes 524288 | tf_op jit(solution)/shard_map/all_to_all | solution.py:85
  177.5 11.5 %copy-start.1 = (f32[8,16384]{1,0:T(8,128)S(1)}, f32[8,16384]{1,0:T(8,128)}, u32[]{:S(2)}) copy-start(f32[8,16384]{1,0:T(8,128)} %param.20) | copy-start | bytes 1572868
  178.6 29.8 %all-to-all-start.5 = ((bf16[512,8,128]{2,1,0:T(8,128)(2,1)}), bf16[512,8,128]{2,1,0:T(8,128)(2,1)}, u32[]{:S(2)}, u32[]{:S(2)}) async-start(bf16[512,8,128]{2,1,0:T(8,128)(2,1)} %convert_element_type.87), calls=%async_computation.5 | async-start | bytes 2097152 | tf_op jit(solution)/shard_map/all_to_all | solution.py:62
  189.3 19.1 %copy-start = (f32[8,128,128]{1,2,0:T(8,128)S(1)}, f32[8,128,128]{1,2,0:T(8,128)}, u32[]{:S(2)}) copy-start(f32[8,128,128]{1,2,0:T(8,128)} %get-tuple-element.34) | copy-start | bytes 1572868
